TPU v7x, 32 devices: a whole 2x2x4 slice. The times are simulated.
32 devices in a mesh: groups: 2 (over x), slab: 16 (over z, y, core).
Axes of the slice: x: 2, y: 2, z: 4, core: 2. Of those that a mesh axis runs over, the one named last changes fastest.
Arguments:
- activations: bfloat16 [2048, 65536], P(('groups', 'slab')), parts along dimension 0, may hold values from 0 to 4
- weights: bfloat16 [6, 2, 512, 128, 128], P(None, None, 'slab'), may hold values from -0.5 to 0.5
- biases: float32 [6, 65536], P(None, 'slab'), may hold values from -1 to 0.5
- columns: int32 [6, 512], P(None, 'slab'), may hold values from 0 to 31
Outputs:
- features: bfloat16 [2048, 65536], P(('groups', 'slab')), parts along dimension 0
There are 2 independent parts, one for each index of `groups`. A program takes and returns all parts, laid end to end along the dimension named above; an argument that names none is the same for every part. Nothing has to cross between parts.
Inputs may be any that keep to these rules, and one draw needn't show every extreme that they name: columns name a block within a group of 32 consecutive blocks.
All inputs are finite; a program needn't handle non-finite values.
Results may differ from a plain program's by a relative error of at most 0.0072.
Values may be sent and summed in bfloat16 or wider, within the bound.
No kernel may reach another device: no remote copies, remote signals or barrier semaphores. Data moves between devices by JAX's collectives and lax.ppermute only.
A program may use at most 128 MiB of HBM per device.

v0:
```python
import jax
import jax.numpy as jnp
from jax import lax
from jax.sharding import PartitionSpec as P

ceiling = 4.0


def from_partner(block, axis, bit):
    count = lax.axis_size(axis)
    route = []
    for low in range(count):
        high = low | 1 << bit
        if high != low and high < count:
            route += [(low, high), (high, low)]
    return lax.ppermute(block, axis, route)


def section_bit(section, remote, log_count):
    return (remote - 1 - section) * (log_count - 1) // (remote - 1)


def local(activations, weights, biases, columns):
    slab_count = lax.axis_size("slab")
    log_count = slab_count.bit_length() - 1
    layer_count = weights.shape[0]
    per_device = weights.shape[2]
    block_width = weights.shape[3]
    local_rows = activations.shape[0]
    remote = (layer_count + 1) // 2
    grouped = activations.reshape(local_rows, slab_count, per_device * block_width)
    stride = 1 << section_bit(0, remote, log_count)
    flipped = grouped.reshape(
        local_rows, slab_count // (2 * stride), 2, stride, per_device * block_width
    )
    flipped = flipped[:, :, ::-1].reshape(local_rows, slab_count, per_device * block_width)
    paired = jnp.stack([grouped, flipped], axis=2)
    arrived = lax.all_to_all(paired, "slab", split_axis=1, concat_axis=0, tiled=True)
    current = arrived[:, 0, 0].reshape(-1, per_device, block_width)
    first_cross = arrived[:, 0, 1].reshape(-1, per_device, block_width)
    for layer_index in range(layer_count):
        if layer_index % 2 == 0:
            if layer_index == 0 and first_cross is not None:
                source = first_cross
            else:
                source = from_partner(
                    current, "slab", section_bit(layer_index // 2, remote, log_count)
                )
        else:
            source = current
        crossing = jnp.take(source, columns[layer_index], axis=1)
        summed = jnp.einsum(
            "rkb,kbc->rkc", current, weights[layer_index, 0], preferred_element_type=jnp.float32
        )
        summed = summed + jnp.einsum(
            "rkb,kbc->rkc", crossing, weights[layer_index, 1], preferred_element_type=jnp.float32
        )
        summed = summed + biases[layer_index].reshape(per_device, block_width)
        current = jnp.clip(summed, 0.0, ceiling).astype(jnp.bfloat16)
    flattened = current.reshape(current.shape[0], per_device * block_width)
    return lax.all_to_all(flattened, "slab", split_axis=0, concat_axis=1, tiled=True)


def solution(mesh):
    placed = (
        P(("groups", "slab"), None),
        P(None, None, "slab", None, None),
        P(None, "slab"),
        P(None, "slab"),
    )
    return jax.shard_map(
        local, mesh=mesh, in_specs=placed, out_specs=P(("groups", "slab"), None), check_vma=False
    )
```

profile of v0, /device:TPU:1, one launch (start us, length us, event | category | flops | bytes accessed | tf_op | source)
XLA Modules:
  0.0 1066.5 jit_solution(5412748452448401006)
XLA Ops:
  0.0 12.1 %copy.28 = bf16[8,8,16,4096]{3,2,1,0:T(8,128)(2,1)} copy(bf16[8,8,16,4096]{3,1,2,0:T(8,128)(2,1)} %bitcast.134) | data formatting | bytes 16777216
  12.1 7.7 reverse_bitcast_fusion
  19.9 8.0 pad_maximum_fusion
  27.9 21.4 %copy.18 = bf16[64,16,2,4096]{3,0,2,1:T(8,128)(2,1)} copy(bf16[64,16,2,4096]{3,1,0,2:T(8,128)(2,1)S(1)} %pad_maximum_fusion) | data formatting | bytes 33554432 | tf_op jit(solution)/shard_map/stack | solution.py:37
  49.2 0.0 copy-start.2
  49.2 0.0 copy-start
  49.2 8.1 all-to-all-start
  57.4 0.0 copy-done.2
  57.4 0.5 compare_and_fusion
  57.9 0.0 copy-done
  57.9 0.7 fusion.79
  58.6 295.9 %all-to-all-done = bf16[64,16,2,4096]{3,0,2,1:T(8,128)(2,1)} async-done(((bf16[64,16,2,4096]{3,0,2,1:T(8,128)(2,1)}), bf16[64,16,2,4096]{3,0,2,1:T(8,128)(2,1)}, u32[]{:S(2)}, u32[]{:S(2)}) %all-to-all-start) | async-done | bytes 16777248 | tf_op jit(solution)/shard_map/all_to_all | solution.py:38
  354.5 8.3 copy.19
  362.7 6.4 fusion.78
  369.2 12.0 %copy.22 = bf16[1024,1,1,4096]{0,3,2,1:T(8,128)(2,1)} copy(bf16[1024,1,1,4096]{3,0,2,1:T(8,128)(2,1)} %get-tuple-element.18) | data formatting | bytes 16777216 | tf_op jit(solution)/shard_map/slice | solution.py:40
  381.1 11.4 %copy.23 = bf16[1024,32,128]{2,0,1:T(8,128)(2,1)} copy(bf16[1024,32,128]{0,2,1:T(8,128)(2,1)} %bitcast.132) | data formatting | bytes 16777216 | tf_op jit(solution)/shard_map/reshape;squeeze | solution.py:40
  392.5 11.9 %copy.20 = bf16[1024,1,1,4096]{0,3,2,1:T(8,128)(2,1)} copy(bf16[1024,1,1,4096]{3,0,2,1:T(8,128)(2,1)} %get-tuple-element.19) | data formatting | bytes 16777216 | tf_op jit(solution)/shard_map/slice | solution.py:39
  404.4 8.4 gather_fusion
  412.8 11.8 %fusion.58 = f32[32,1024,128]{2,1,0:T(8,128)} fusion(bf16[1024,32,128]{0,2,1:T(8,128)(2,1)} %bitcast.131, bf16[6,2,32,128,128]{4,3,2,1,0:T(8,128)(2,1)} %param.7), kind=kOutput, calls=%fused_computation.60 | convolution fusion | flops 1073741824 | bytes 26214400 | tf_op jit(solution)/shard_map/rkb,kbc->rkc/dot_general | solution.py:52
  424.6 13.5 %fusion.18 = bf16[1024,32,128]{2,0,1:T(8,128)(2,1)} fusion(f32[32,128]{1,0:T(8,128)S(1)} %bitcast.140, f32[32,1024,128]{2,1,0:T(8,128)} %fusion.58, bf16[32,1024,128]{2,1,0:T(8,128)(2,1)} %gather_fusion, pred[32]{0:T(512)(128)(4,1)S(1)} %get-tuple-element.32, bf16[6,2,32,128,128]{4,3,2,1,0:T(8,128)(2,1)} %param.7), kind=kOutput, calls=%fused_computation.32 | convolution fusion | flops 1094713344 | bytes 34619424 | tf_op jit(solution)/shard_map/rkb,kbc->rkc/dot_general | solution.py:55
  438.2 11.7 %fusion.55 = f32[32,1024,128]{2,1,0:T(8,128)} fusion(bf16[1024,32,128]{2,0,1:T(8,128)(2,1)} %fusion.18, bf16[6,2,32,128,128]{4,3,2,1,0:T(8,128)(2,1)} %param.7), kind=kOutput, calls=%fused_computation.57 | convolution fusion | flops 1073741824 | bytes 26214400 | tf_op jit(solution)/shard_map/rkb,kbc->rkc/dot_general | solution.py:52
  449.8 8.4 gather_fusion.1
  458.2 13.7 %fusion.21 = bf16[1024,32,128]{2,0,1:T(8,128)(2,1)} fusion(f32[32,128]{1,0:T(8,128)S(1)} %bitcast.139, f32[32,1024,128]{2,1,0:T(8,128)} %fusion.55, bf16[32,1024,128]{2,1,0:T(8,128)(2,1)} %gather_fusion.1, pred[32]{0:T(512)(128)(4,1)S(1)} %get-tuple-element.30, bf16[6,2,32,128,128]{4,3,2,1,0:T(8,128)(2,1)} %param.7), kind=kOutput, calls=%fused_computation.33 | convolution fusion | flops 1094713344 | bytes 34619424 | tf_op jit(solution)/shard_map/rkb,kbc->rkc/dot_general | solution.py:55
  471.9 22.8 %collective-permute-start = (bf16[1024,32,128]{2,0,1:T(8,128)(2,1)}, bf16[1024,32,128]{2,0,1:T(8,128)(2,1)}, u32[]{:S(2)}, u32[]{:S(2)}) collective-permute-start(bf16[1024,32,128]{2,0,1:T(8,128)(2,1)} %fusion.21), channel_id=1, source_target_pairs={{0,2},{2,0},{1,3},{3,1},{4,6},{6,4},{5,7},{7,5},{8,10},{10,8},{9,1... | collective-permute-start | bytes 25165832 | tf_op jit(solution)/shard_map/ppermute | solution.py:16
  494.7 11.7 %fusion.52 = f32[32,1024,128]{2,1,0:T(8,128)} fusion(bf16[1024,32,128]{2,0,1:T(8,128)(2,1)} %fusion.21, bf16[6,2,32,128,128]{4,3,2,1,0:T(8,128)(2,1)} %param.7), kind=kOutput, calls=%fused_computation.54 | convolution fusion | flops 1073741824 | bytes 26214400 | tf_op jit(solution)/shard_map/rkb,kbc->rkc/dot_general | solution.py:52
  506.4 169.1 %collective-permute-done = bf16[1024,32,128]{2,0,1:T(8,128)(2,1)} collective-permute-done((bf16[1024,32,128]{2,0,1:T(8,128)(2,1)}, bf16[1024,32,128]{2,0,1:T(8,128)(2,1)}, u32[]{:S(2)}, u32[]{:S(2)}) %collective-permute-start) | collective-permute-done | bytes 8388640 | tf_op jit(solution)/shard_map/ppermute | solution.py:16
  675.5 8.6 gather_fusion.2
  684.1 13.5 %fusion.24 = bf16[1024,32,128]{2,0,1:T(8,128)(2,1)} fusion(f32[32,128]{1,0:T(8,128)S(1)} %bitcast.138, f32[32,1024,128]{2,1,0:T(8,128)} %fusion.52, bf16[32,1024,128]{2,1,0:T(8,128)(2,1)} %gather_fusion.2, pred[32]{0:T(512)(128)(4,1)S(1)} %get-tuple-element.28, bf16[6,2,32,128,128]{4,3,2,1,0:T(8,128)(2,1)} %param.7), kind=kOutput, calls=%fused_computation.34 | convolution fusion | flops 1094713344 | bytes 34619424 | tf_op jit(solution)/shard_map/rkb,kbc->rkc/dot_general | solution.py:55
  697.6 11.7 %fusion.49 = f32[32,1024,128]{2,1,0:T(8,128)} fusion(bf16[1024,32,128]{2,0,1:T(8,128)(2,1)} %fusion.24, bf16[6,2,32,128,128]{4,3,2,1,0:T(8,128)(2,1)} %param.7), kind=kOutput, calls=%fused_computation.51 | convolution fusion | flops 1073741824 | bytes 26214400 | tf_op jit(solution)/shard_map/rkb,kbc->rkc/dot_general | solution.py:52
  709.3 8.5 gather_fusion.3
  717.8 13.5 %fusion.27 = bf16[1024,32,128]{2,0,1:T(8,128)(2,1)} fusion(f32[32,128]{1,0:T(8,128)S(1)} %bitcast.137, f32[32,1024,128]{2,1,0:T(8,128)} %fusion.49, bf16[32,1024,128]{2,1,0:T(8,128)(2,1)} %gather_fusion.3, pred[32]{0:T(512)(128)(4,1)S(1)} %get-tuple-element.26, bf16[6,2,32,128,128]{4,3,2,1,0:T(8,128)(2,1)} %param.7), kind=kOutput, calls=%fused_computation.35 | convolution fusion | flops 1094713344 | bytes 34619424 | tf_op jit(solution)/shard_map/rkb,kbc->rkc/dot_general | solution.py:55
  731.3 0.4 collective-permute-start.1
  731.7 11.7 %fusion.46 = f32[32,1024,128]{2,1,0:T(8,128)} fusion(bf16[1024,32,128]{2,0,1:T(8,128)(2,1)} %fusion.27, bf16[6,2,32,128,128]{4,3,2,1,0:T(8,128)(2,1)} %param.7), kind=kOutput, calls=%fused_computation.48 | convolution fusion | flops 1073741824 | bytes 26214400 | tf_op jit(solution)/shard_map/rkb,kbc->rkc/dot_general | solution.py:52
  743.4 1.4 collective-permute-done.1
  744.8 8.8 gather_fusion.4
  753.6 13.5 %fusion.30 = bf16[1024,32,128]{2,0,1:T(8,128)(2,1)} fusion(f32[32,128]{1,0:T(8,128)S(1)} %bitcast.136, f32[32,1024,128]{2,1,0:T(8,128)} %fusion.46, bf16[32,1024,128]{2,1,0:T(8,128)(2,1)} %gather_fusion.4, pred[32]{0:T(512)(128)(4,1)S(1)} %get-tuple-element.34, bf16[6,2,32,128,128]{4,3,2,1,0:T(8,128)(2,1)} %param.7), kind=kOutput, calls=%fused_computation.36 | convolution fusion | flops 1094713344 | bytes 34619424 | tf_op jit(solution)/shard_map/rkb,kbc->rkc/dot_general | solution.py:55
  767.1 11.7 %fusion.43 = f32[32,1024,128]{2,1,0:T(8,128)} fusion(bf16[1024,32,128]{2,0,1:T(8,128)(2,1)} %fusion.30, bf16[6,2,32,128,128]{4,3,2,1,0:T(8,128)(2,1)} %param.7), kind=kOutput, calls=%fused_computation.45 | convolution fusion | flops 1073741824 | bytes 26214400 | tf_op jit(solution)/shard_map/rkb,kbc->rkc/dot_general | solution.py:52
  778.8 0.0 copy-start.1
  778.8 0.0 copy-start.3
  778.8 8.6 gather_fusion.5
  787.4 0.0 copy-done.1
  787.4 0.0 copy-done.3
  787.4 13.7 %fusion.33 = bf16[1024,32,128]{2,0,1:T(8,128)(2,1)} fusion(f32[32,128]{1,0:T(8,128)S(1)} %bitcast.135, f32[32,1024,128]{2,1,0:T(8,128)} %fusion.43, bf16[32,1024,128]{2,1,0:T(8,128)(2,1)} %gather_fusion.5, pred[32]{0:T(512)(128)(4,1)S(1)} %copy-done.3, bf16[6,2,32,128,128]{4,3,2,1,0:T(8,128)(2,1)} %param.7), kind=kOutput, calls=%fused_computation.37 | convolution fusion | flops 1094713344 | bytes 34619424 | tf_op jit(solution)/shard_map/rkb,kbc->rkc/dot_general | solution.py:55
  801.1 12.2 %copy.24 = bf16[1024,32,128]{2,1,0:T(8,128)(2,1)} copy(bf16[1024,32,128]{2,0,1:T(8,128)(2,1)} %fusion.33) | data formatting | bytes 16777216 | tf_op jit(solution)/shard_map/convert_element_type | solution.py:59
  813.3 13.3 %all_to_all.31 = bf16[16,64,4096]{2,1,0:T(8,128)(2,1)} reshape(bf16[1024,32,128]{2,1,0:T(8,128)(2,1)} %copy.24) | data formatting | bytes 16777216 | tf_op jit(solution)/shard_map/all_to_all | solution.py:61
  826.6 231.7 %all_to_all.37 = bf16[16,64,4096]{2,1,0:T(8,128)(2,1)} all-to-all(bf16[16,64,4096]{2,1,0:T(8,128)(2,1)} %all_to_all.31), channel_id=1, replica_groups=mesh['groups'=2,'slab'=16] {'slab'}, dimensions={0} | all-to-all | bytes 16777216 | tf_op jit(solution)/shard_map/all_to_all | solution.py:61
  1058.4 7.9 copy.27
  (3 shorter events, 0.0 us)
Async XLA Ops:
  49.2 8.2 copy-start.2
  49.2 8.7 copy-start
  49.2 305.2 %all-to-all-start = ((bf16[64,16,2,4096]{3,0,2,1:T(8,128)(2,1)}), bf16[64,16,2,4096]{3,0,2,1:T(8,128)(2,1)}, u32[]{:S(2)}, u32[]{:S(2)}) async-start(bf16[64,16,2,4096]{3,0,2,1:T(8,128)(2,1)} %copy.18), calls=%async_computation | async-start | bytes 33554432 | tf_op jit(solution)/shard_map/all_to_all | solution.py:38
  471.9 203.6 %collective-permute-start = (bf16[1024,32,128]{2,0,1:T(8,128)(2,1)}, bf16[1024,32,128]{2,0,1:T(8,128)(2,1)}, u32[]{:S(2)}, u32[]{:S(2)}) collective-permute-start(bf16[1024,32,128]{2,0,1:T(8,128)(2,1)} %fusion.21), channel_id=1, source_target_pairs={{0,2},{2,0},{1,3},{3,1},{4,6},{6,4},{5,7},{7,5},{8,10},{10,8},{9,1... | collective-permute-start | bytes 25165832 | tf_op jit(solution)/shard_map/ppermute | solution.py:16
  731.3 13.5 %collective-permute-start.1 = (bf16[1024,32,128]{2,0,1:T(8,128)(2,1)}, bf16[1024,32,128]{2,0,1:T(8,128)(2,1)}, u32[]{:S(2)}, u32[]{:S(2)}) collective-permute-start(bf16[1024,32,128]{2,0,1:T(8,128)(2,1)} %fusion.27), channel_id=1, source_target_pairs={{0,1},{1,0},{2,3},{3,2},{4,5},{5,4},{6,7},{7,6},{8,9},{9,8},{10,11... | collective-permute-start | bytes 25165832 | tf_op jit(solution)/shard_map/ppermute | solution.py:16
  778.8 8.6 copy-start.1
  778.8 8.6 copy-start.3
where the time goes:
time: 1070 us
  waiting for transfers between devices  466 us (44%)
  blocking collectives  232 us (22%)
  local copies, waits for them, and re-layouts  177 us (17%)
  matrix products  152 us (14%)
  starting transfers between devices  31.4 us (3%)
    all_to_all x1, waiting for transfers between devices, local(): lax.all_to_all(paired, 'slab', split_axis=1, concat_axis=0, tiled=True)  296 us
    all_to_all x1, blocking collectives, local(): lax.all_to_all(flattened, 'slab', split_axis=0, concat_axis=1, tiled=True)  232 us
    ppermute x2, waiting for transfers between devices, from_partner(): return lax.ppermute(block, axis, route)  171 us
    dot_general x6, matrix products, local(): jnp.einsum('rkb,kbc->rkc', crossing, weights[layer_index, 1], preferred_e...  81.4 us
    dot_general x6, matrix products, local(): jnp.einsum('rkb,kbc->rkc', current, weights[layer_index, 0], preferred_el...  70.2 us
    gather x6, local copies, waits for them, and re-layouts, local(): crossing = jnp.take(source, columns[layer_index], axis=1)  51.3 us
    another operation x2, local copies, waits for them, and re-layouts, local(): paired = jnp.stack([grouped, flipped], axis=2)  29.1 us
    ppermute x2, starting transfers between devices, from_partner(): return lax.ppermute(block, axis, route)  23.2 us
  transfers between devices with their start and end apart: 3, of which 3 were waited for; matrix products, arithmetic and copies ran while one was open for 2% of the time, Pallas kernels for 0%

commit v1 on v0

--- a/solution.py
+++ b/solution.py
@@ -4,6 +4,12 @@
 from jax.sharding import PartitionSpec as P
 
 ceiling = 4.0
+
+
+def swap_blocks(x, name, split, join):
+    pieces = jnp.split(x, lax.axis_size(name), axis=split)
+    received = lax.all_to_all(jnp.stack(pieces), name, 0, 0)
+    return jnp.concatenate(received, axis=join)
 
 
 def from_partner(block, axis, bit):
@@ -58,7 +64,7 @@
         summed = summed + biases[layer_index].reshape(per_device, block_width)
         current = jnp.clip(summed, 0.0, ceiling).astype(jnp.bfloat16)
     flattened = current.reshape(current.shape[0], per_device * block_width)
-    return lax.all_to_all(flattened, "slab", split_axis=0, concat_axis=1, tiled=True)
+    return swap_blocks(flattened, "slab", 0, 1)
 
 
 def solution(mesh):

time: 1070 us -> 1130 us (1.056)
  local copies, waits for them, and re-layouts: 177 us -> 235 us
    another operation x0 -> x17, local copies, waits for them, and re-layouts: none -> 34.2 us  [swap_blocks(): received = lax.all_to_all(jnp.stack(pieces), name, 0, 0)]
    split x0 -> x17, local copies, waits for them, and re-layouts: none -> 33.8 us  [swap_blocks(): pieces = jnp.split(x, lax.axis_size(name), axis=split)]
    all_to_all x2 -> x0, local copies, waits for them, and re-layouts: 21.2 us -> none  [local(): lax.all_to_all(flattened, 'slab', split_axis=0, concat_axis=1, tiled=True)]
    unnamed x9 -> x50, local copies, waits for them, and re-layouts: 12.2 us -> 27.8 us
    convert_element_type x1 -> x0, local copies, waits for them, and re-layouts: 12.2 us -> none  [local(): current = jnp.clip(summed, 0.0, ceiling).astype(jnp.bfloat16)]
where the time goes in v1:
time: 1130 us; the launch traced here: 1120 us
  waiting for transfers between devices  466 us (41%)
  local copies, waits for them, and re-layouts  235 us (21%)
  blocking collectives  232 us (21%)
  matrix products  151 us (13%)
  starting transfers between devices  31 us (3%)
    all_to_all x1, waiting for transfers between devices, local(): lax.all_to_all(paired, 'slab', split_axis=1, concat_axis=0, tiled=True)  296 us
    all_to_all x1, blocking collectives, swap_blocks(): received = lax.all_to_all(jnp.stack(pieces), name, 0, 0)  232 us
    ppermute x2, waiting for transfers between devices, from_partner(): return lax.ppermute(block, axis, route)  171 us
    dot_general x6, matrix products, local(): jnp.einsum('rkb,kbc->rkc', crossing, weights[layer_index, 1], preferred_e...  81.1 us
    dot_general x6, matrix products, local(): jnp.einsum('rkb,kbc->rkc', current, weights[layer_index, 0], preferred_el...  70.1 us
    gather x6, local copies, waits for them, and re-layouts, local(): crossing = jnp.take(source, columns[layer_index], axis=1)  51.6 us
    another operation x17, local copies, waits for them, and re-layouts, swap_blocks(): received = lax.all_to_all(jnp.stack(pieces), name, 0, 0)  34.2 us
    split x17, local copies, waits for them, and re-layouts, swap_blocks(): pieces = jnp.split(x, lax.axis_size(name), axis=split)  33.8 us
  transfers between devices with their start and end apart: 3, of which 3 were waited for; matrix products, arithmetic and copies ran while one was open for 2% of the time, Pallas kernels for 0%

profile of v1, /device:TPU:1, one launch (start us, length us, event | category | flops | bytes accessed | tf_op | source)
XLA Modules:
  0.0 1124.3 jit_solution(4854934554945823288)
XLA Ops:
  0.0 12.1 %copy.73 = bf16[8,8,16,4096]{3,2,1,0:T(8,128)(2,1)} copy(bf16[8,8,16,4096]{3,1,2,0:T(8,128)(2,1)} %bitcast.134) | data formatting | bytes 16777216
  12.1 7.8 reverse_bitcast_fusion
  19.9 8.0 pad_maximum_fusion
  27.9 21.4 %copy.48 = bf16[64,16,2,4096]{3,0,2,1:T(8,128)(2,1)} copy(bf16[64,16,2,4096]{3,1,0,2:T(8,128)(2,1)S(1)} %pad_maximum_fusion) | data formatting | bytes 33554432 | tf_op jit(solution)/shard_map/stack | solution.py:43
  49.3 7.8 all-to-all-start
  58.4 295.8 %all-to-all-done = bf16[64,16,2,4096]{3,0,2,1:T(8,128)(2,1)} async-done(((bf16[64,16,2,4096]{3,0,2,1:T(8,128)(2,1)}), bf16[64,16,2,4096]{3,0,2,1:T(8,128)(2,1)}, u32[]{:S(2)}, u32[]{:S(2)}) %all-to-all-start) | async-done | bytes 16777248 | tf_op jit(solution)/shard_map/all_to_all | solution.py:44
  354.2 8.3 copy.49
  362.5 6.5 fusion.78
  368.9 12.0 %copy.52 = bf16[1024,1,1,4096]{0,3,2,1:T(8,128)(2,1)} copy(bf16[1024,1,1,4096]{3,0,2,1:T(8,128)(2,1)} %get-tuple-element.18) | data formatting | bytes 16777216 | tf_op jit(solution)/shard_map/slice | solution.py:46
  380.9 11.4 %copy.53 = bf16[1024,32,128]{2,0,1:T(8,128)(2,1)} copy(bf16[1024,32,128]{0,2,1:T(8,128)(2,1)} %bitcast.132) | data formatting | bytes 16777216 | tf_op jit(solution)/shard_map/reshape;squeeze | solution.py:46
  392.3 11.9 %copy.50 = bf16[1024,1,1,4096]{0,3,2,1:T(8,128)(2,1)} copy(bf16[1024,1,1,4096]{3,0,2,1:T(8,128)(2,1)} %get-tuple-element.19) | data formatting | bytes 16777216 | tf_op jit(solution)/shard_map/slice | solution.py:45
  404.3 8.4 gather_fusion
  412.7 11.8 %fusion.58 = f32[32,1024,128]{2,1,0:T(8,128)} fusion(bf16[1024,32,128]{0,2,1:T(8,128)(2,1)} %bitcast.131, bf16[6,2,32,128,128]{4,3,2,1,0:T(8,128)(2,1)} %param.7), kind=kOutput, calls=%fused_computation.60 | convolution fusion | flops 1073741824 | bytes 26214400 | tf_op jit(solution)/shard_map/rkb,kbc->rkc/dot_general | solution.py:58
  424.5 13.5 %fusion.18 = bf16[1024,32,128]{2,0,1:T(8,128)(2,1)} fusion(f32[32,128]{1,0:T(8,128)S(1)} %bitcast.140, f32[32,1024,128]{2,1,0:T(8,128)} %fusion.58, bf16[32,1024,128]{2,1,0:T(8,128)(2,1)} %gather_fusion, pred[32]{0:T(512)(128)(4,1)S(1)} %get-tuple-element.48, bf16[6,2,32,128,128]{4,3,2,1,0:T(8,128)(2,1)} %param.7), kind=kOutput, calls=%fused_computation.32 | convolution fusion | flops 1094713344 | bytes 34619424 | tf_op jit(solution)/shard_map/rkb,kbc->rkc/dot_general | solution.py:61
  438.0 11.7 %fusion.55 = f32[32,1024,128]{2,1,0:T(8,128)} fusion(bf16[1024,32,128]{2,0,1:T(8,128)(2,1)} %fusion.18, bf16[6,2,32,128,128]{4,3,2,1,0:T(8,128)(2,1)} %param.7), kind=kOutput, calls=%fused_computation.57 | convolution fusion | flops 1073741824 | bytes 26214400 | tf_op jit(solution)/shard_map/rkb,kbc->rkc/dot_general | solution.py:58
  449.7 8.4 gather_fusion.1
  458.1 13.7 %fusion.21 = bf16[1024,32,128]{2,0,1:T(8,128)(2,1)} fusion(f32[32,128]{1,0:T(8,128)S(1)} %bitcast.139, f32[32,1024,128]{2,1,0:T(8,128)} %fusion.55, bf16[32,1024,128]{2,1,0:T(8,128)(2,1)} %gather_fusion.1, pred[32]{0:T(512)(128)(4,1)S(1)} %get-tuple-element.46, bf16[6,2,32,128,128]{4,3,2,1,0:T(8,128)(2,1)} %param.7), kind=kOutput, calls=%fused_computation.33 | convolution fusion | flops 1094713344 | bytes 34619424 | tf_op jit(solution)/shard_map/rkb,kbc->rkc/dot_general | solution.py:61
  471.8 22.8 %collective-permute-start = (bf16[1024,32,128]{2,0,1:T(8,128)(2,1)}, bf16[1024,32,128]{2,0,1:T(8,128)(2,1)}, u32[]{:S(2)}, u32[]{:S(2)}) collective-permute-start(bf16[1024,32,128]{2,0,1:T(8,128)(2,1)} %fusion.21), channel_id=1, source_target_pairs={{0,2},{2,0},{1,3},{3,1},{4,6},{6,4},{5,7},{7,5},{8,10},{10,8},{9,1... | collective-permute-start | bytes 25165832 | tf_op jit(solution)/shard_map/ppermute | solution.py:22
  494.6 11.7 %fusion.52 = f32[32,1024,128]{2,1,0:T(8,128)} fusion(bf16[1024,32,128]{2,0,1:T(8,128)(2,1)} %fusion.21, bf16[6,2,32,128,128]{4,3,2,1,0:T(8,128)(2,1)} %param.7), kind=kOutput, calls=%fused_computation.54 | convolution fusion | flops 1073741824 | bytes 26214400 | tf_op jit(solution)/shard_map/rkb,kbc->rkc/dot_general | solution.py:58
  506.3 169.1 %collective-permute-done = bf16[1024,32,128]{2,0,1:T(8,128)(2,1)} collective-permute-done((bf16[1024,32,128]{2,0,1:T(8,128)(2,1)}, bf16[1024,32,128]{2,0,1:T(8,128)(2,1)}, u32[]{:S(2)}, u32[]{:S(2)}) %collective-permute-start) | collective-permute-done | bytes 8388640 | tf_op jit(solution)/shard_map/ppermute | solution.py:22
  675.4 8.6 gather_fusion.2
  684.0 13.5 %fusion.24 = bf16[1024,32,128]{2,0,1:T(8,128)(2,1)} fusion(f32[32,128]{1,0:T(8,128)S(1)} %bitcast.138, f32[32,1024,128]{2,1,0:T(8,128)} %fusion.52, bf16[32,1024,128]{2,1,0:T(8,128)(2,1)} %gather_fusion.2, pred[32]{0:T(512)(128)(4,1)S(1)} %get-tuple-element.44, bf16[6,2,32,128,128]{4,3,2,1,0:T(8,128)(2,1)} %param.7), kind=kOutput, calls=%fused_computation.34 | convolution fusion | flops 1094713344 | bytes 34619424 | tf_op jit(solution)/shard_map/rkb,kbc->rkc/dot_general | solution.py:61
  697.5 11.7 %fusion.49 = f32[32,1024,128]{2,1,0:T(8,128)} fusion(bf16[1024,32,128]{2,0,1:T(8,128)(2,1)} %fusion.24, bf16[6,2,32,128,128]{4,3,2,1,0:T(8,128)(2,1)} %param.7), kind=kOutput, calls=%fused_computation.51 | convolution fusion | flops 1073741824 | bytes 26214400 | tf_op jit(solution)/shard_map/rkb,kbc->rkc/dot_general | solution.py:58
  709.1 8.5 gather_fusion.3
  717.7 13.5 %fusion.27 = bf16[1024,32,128]{2,0,1:T(8,128)(2,1)} fusion(f32[32,128]{1,0:T(8,128)S(1)} %bitcast.137, f32[32,1024,128]{2,1,0:T(8,128)} %fusion.49, bf16[32,1024,128]{2,1,0:T(8,128)(2,1)} %gather_fusion.3, pred[32]{0:T(512)(128)(4,1)S(1)} %get-tuple-element.42, bf16[6,2,32,128,128]{4,3,2,1,0:T(8,128)(2,1)} %param.7), kind=kOutput, calls=%fused_computation.35 | convolution fusion | flops 1094713344 | bytes 34619424 | tf_op jit(solution)/shard_map/rkb,kbc->rkc/dot_general | solution.py:61
  731.6 11.7 %fusion.46 = f32[32,1024,128]{2,1,0:T(8,128)} fusion(bf16[1024,32,128]{2,0,1:T(8,128)(2,1)} %fusion.27, bf16[6,2,32,128,128]{4,3,2,1,0:T(8,128)(2,1)} %param.7), kind=kOutput, calls=%fused_computation.48 | convolution fusion | flops 1073741824 | bytes 26214400 | tf_op jit(solution)/shard_map/rkb,kbc->rkc/dot_general | solution.py:58
  743.2 1.5 collective-permute-done.1
  744.7 9.0 gather_fusion.4
  753.6 13.5 %fusion.30 = bf16[1024,32,128]{2,0,1:T(8,128)(2,1)} fusion(f32[32,128]{1,0:T(8,128)S(1)} %bitcast.136, f32[32,1024,128]{2,1,0:T(8,128)} %fusion.46, bf16[32,1024,128]{2,1,0:T(8,128)(2,1)} %gather_fusion.4, pred[32]{0:T(512)(128)(4,1)S(1)} %get-tuple-element.50, bf16[6,2,32,128,128]{4,3,2,1,0:T(8,128)(2,1)} %param.7), kind=kOutput, calls=%fused_computation.36 | convolution fusion | flops 1094713344 | bytes 34619424 | tf_op jit(solution)/shard_map/rkb,kbc->rkc/dot_general | solution.py:61
  767.1 11.7 %fusion.43 = f32[32,1024,128]{2,1,0:T(8,128)} fusion(bf16[1024,32,128]{2,0,1:T(8,128)(2,1)} %fusion.30, bf16[6,2,32,128,128]{4,3,2,1,0:T(8,128)(2,1)} %param.7), kind=kOutput, calls=%fused_computation.45 | convolution fusion | flops 1073741824 | bytes 26214400 | tf_op jit(solution)/shard_map/rkb,kbc->rkc/dot_general | solution.py:58
  778.8 8.6 gather_fusion.5
  787.4 13.5 %fusion.33 = bf16[1024,32,128]{2,0,1:T(8,128)(2,1)} fusion(f32[32,128]{1,0:T(8,128)S(1)} %bitcast.135, f32[32,1024,128]{2,1,0:T(8,128)} %fusion.43, bf16[32,1024,128]{2,1,0:T(8,128)(2,1)} %gather_fusion.5, pred[32]{0:T(512)(128)(4,1)S(1)} %copy-done.16, bf16[6,2,32,128,128]{4,3,2,1,0:T(8,128)(2,1)} %param.7), kind=kOutput, calls=%fused_computation.37 | convolution fusion | flops 1094713344 | bytes 34619424 | tf_op jit(solution)/shard_map/rkb,kbc->rkc/dot_general | solution.py:61
  800.8 6.1 fusion.79
  808.1 2.1 stack.55
  810.1 1.9 constant_dynamic-update-slice_fusion.15
  812.0 2.2 copy.55
  814.2 2.1 stack.56
  816.3 2.2 copy.56
  818.4 2.1 stack.57
  820.5 2.2 copy.57
  822.7 2.1 stack.58
  824.8 2.2 copy.58
  826.9 2.1 stack.59
  829.0 2.2 copy.59
  831.2 2.1 stack.60
  833.2 2.2 copy.60
  835.4 2.1 stack.61
  837.5 2.2 copy.61
  839.7 2.1 stack.62
  841.7 2.2 copy.62
  843.9 2.1 stack.63
  846.0 2.2 copy.63
  848.2 2.1 stack.64
  851.4 2.1 stack.65
  854.6 2.1 stack.66
  857.9 2.1 stack.67
  861.1 2.1 stack.68
  864.4 2.1 stack.69
  866.5 1.2 copy.69
  867.7 2.1 stack.70
  873.2 1.9 constant_dynamic-update-slice_fusion.10
  875.9 1.9 constant_dynamic-update-slice_fusion.8
  884.5 231.8 %all_to_all.23 = bf16[16,64,4096]{2,1,0:T(8,128)(2,1)} all-to-all(bf16[16,64,4096]{2,1,0:T(8,128)(2,1)} %constant_dynamic-update-slice_fusion), channel_id=1, replica_groups=mesh['groups'=2,'slab'=16] {'slab'}, dimensions={0} | all-to-all | bytes 16777216 | tf_op jit(solution)/shard_map/all_to_all | solution.py:11
  1116.2 7.9 copy.72
  (59 shorter events, 19.4 us)
Async XLA Ops:
  49.3 7.8 copy-start.15
  49.3 8.4 copy-start.13
  49.3 304.9 %all-to-all-start = ((bf16[64,16,2,4096]{3,0,2,1:T(8,128)(2,1)}), bf16[64,16,2,4096]{3,0,2,1:T(8,128)(2,1)}, u32[]{:S(2)}, u32[]{:S(2)}) async-start(bf16[64,16,2,4096]{3,0,2,1:T(8,128)(2,1)} %copy.48), calls=%async_computation | async-start | bytes 33554432 | tf_op jit(solution)/shard_map/all_to_all | solution.py:44
  471.8 203.6 %collective-permute-start = (bf16[1024,32,128]{2,0,1:T(8,128)(2,1)}, bf16[1024,32,128]{2,0,1:T(8,128)(2,1)}, u32[]{:S(2)}, u32[]{:S(2)}) collective-permute-start(bf16[1024,32,128]{2,0,1:T(8,128)(2,1)} %fusion.21), channel_id=1, source_target_pairs={{0,2},{2,0},{1,3},{3,1},{4,6},{6,4},{5,7},{7,5},{8,10},{10,8},{9,1... | collective-permute-start | bytes 25165832 | tf_op jit(solution)/shard_map/ppermute | solution.py:22
  731.1 13.5 %collective-permute-start.1 = (bf16[1024,32,128]{2,0,1:T(8,128)(2,1)}, bf16[1024,32,128]{2,0,1:T(8,128)(2,1)}, u32[]{:S(2)}, u32[]{:S(2)}) collective-permute-start(bf16[1024,32,128]{2,0,1:T(8,128)(2,1)} %fusion.27), channel_id=1, source_target_pairs={{0,1},{1,0},{2,3},{3,2},{4,5},{5,4},{6,7},{7,6},{8,9},{9,8},{10,11... | collective-permute-start | bytes 25165832 | tf_op jit(solution)/shard_map/ppermute | solution.py:22
  778.8 8.6 copy-start.14
  778.8 8.6 copy-start.16
  851.4 18.5 %copy-start = (bf16[1,64,4096]{2,1,0:T(8,128)(2,1)S(1)}, bf16[1,64,4096]{2,1,0:T(8,128)(2,1)}, u32[]{:S(2)}) copy-start(bf16[1,64,4096]{2,1,0:T(8,128)(2,1)} %stack.56) | copy-start | bytes 1572868
  854.6 16.1 %copy-start.1 = (bf16[1,64,4096]{2,1,0:T(8,128)(2,1)S(1)}, bf16[1,64,4096]{2,1,0:T(8,128)(2,1)}, u32[]{:S(2)}) copy-start(bf16[1,64,4096]{2,1,0:T(8,128)(2,1)} %stack.57) | copy-start | bytes 1572868
  857.9 13.7 %copy-start.2 = (bf16[1,64,4096]{2,1,0:T(8,128)(2,1)S(1)}, bf16[1,64,4096]{2,1,0:T(8,128)(2,1)}, u32[]{:S(2)}) copy-start(bf16[1,64,4096]{2,1,0:T(8,128)(2,1)} %stack.58) | copy-start | bytes 1572868
  861.1 11.2 %copy-start.3 = (bf16[1,64,4096]{2,1,0:T(8,128)(2,1)S(1)}, bf16[1,64,4096]{2,1,0:T(8,128)(2,1)}, u32[]{:S(2)}) copy-start(bf16[1,64,4096]{2,1,0:T(8,128)(2,1)} %stack.59) | copy-start | bytes 1572868
  864.4 10.7 copy-start.4
  867.7 10.1 copy-start.5
  869.8 8.8 copy-start.6
  869.8 9.6 copy-start.7
  869.8 10.4 copy-start.8
  869.9 11.3 %copy-start.9 = (bf16[1,64,4096]{2,1,0:T(8,128)(2,1)S(1)}, bf16[1,64,4096]{2,1,0:T(8,128)(2,1)}, u32[]{:S(2)}) copy-start(bf16[1,64,4096]{2,1,0:T(8,128)(2,1)} %stack.67) | copy-start | bytes 1572868
  869.9 12.1 %copy-start.10 = (bf16[1,64,4096]{2,1,0:T(8,128)(2,1)S(1)}, bf16[1,64,4096]{2,1,0:T(8,128)(2,1)}, u32[]{:S(2)}) copy-start(bf16[1,64,4096]{2,1,0:T(8,128)(2,1)} %stack.68) | copy-start | bytes 1572868
  869.9 12.9 %copy-start.11 = (bf16[1,64,4096]{2,1,0:T(8,128)(2,1)S(1)}, bf16[1,64,4096]{2,1,0:T(8,128)(2,1)}, u32[]{:S(2)}) copy-start(bf16[1,64,4096]{2,1,0:T(8,128)(2,1)} %stack.69) | copy-start | bytes 1572868
  869.9 13.7 %copy-start.12 = (bf16[1,64,4096]{2,1,0:T(8,128)(2,1)S(1)}, bf16[1,64,4096]{2,1,0:T(8,128)(2,1)}, u32[]{:S(2)}) copy-start(bf16[1,64,4096]{2,1,0:T(8,128)(2,1)} %stack.70) | copy-start | bytes 1572868
